TPU v7x, 32 devices: a whole 2x2x4 slice. The times are simulated.
32 devices in a mesh: cam: 2 (over core), tile: 16 (over z, y, x).
Axes of the slice: x: 2, y: 2, z: 4, core: 2. Of those that a mesh axis runs over, the one named last changes fastest.
Arguments:
- queries: bfloat16 [4096, 256], P('tile'), as said below
- keys: bfloat16 [2048, 256], P(('cam', 'tile')), as said below
- values: bfloat16 [2048, 256], P(('cam', 'tile')), may hold values from -6 to 6
- grad_out: bfloat16 [4096, 256], P('tile'), may hold values from -6 to 6
- visible: int32 [32, 64], P('tile', 'cam'), may hold values from 0 to 1, as said below
- counts: int32 [64], P('cam'), may hold values from 2 to 32
Outputs:
- grad_queries: bfloat16 [4096, 256], P('tile')
- grad_keys: bfloat16 [2048, 256], P(('cam', 'tile'))
- grad_values: bfloat16 [2048, 256], P(('cam', 'tile'))
Inputs may be any that keep to these rules, and one draw needn't show every extreme that they name: Every tile has at least one visible block. `queries`: projected query features. `keys`: projected key features.
All inputs are finite; a program needn't handle non-finite values.
Results may differ from a plain program's by a relative error of at most 0.0052.
Values may be sent and summed in bfloat16 or wider, within the bound.
No kernel may reach another device: no remote copies, remote signals or barrier semaphores. Data moves between devices by JAX's collectives and lax.ppermute only.
A program may use at most 128 MiB of HBM per device.

v0:
```python
import math
import jax
import jax.numpy as jnp
from jax import lax
from jax.sharding import PartitionSpec as P

H = 8


def merged(array, axis, combine):
    everything = jax.tree.map(lambda part: lax.all_gather(part, axis), array)
    initial = jax.tree.map(lambda part: part[0], everything)

    def step(k, so_far):
        return combine(so_far, jax.tree.map(lambda part: part[k], everything))

    return lax.fori_loop(1, lax.axis_size(axis), step, initial)


def combine_stats(first, second):
    top = jnp.maximum(first[0], second[0])
    total = first[1] * jnp.exp(first[0] - top) + second[1] * jnp.exp(second[0] - top)
    return (top, total)


def shards(queries, keys, values, grad_out, visible, counts):
    row_count, width = queries.shape
    head_dim = width // H
    scale = 1.0 / math.sqrt(head_dim)
    key_all, value_all = (
        lax.all_gather(keys, "tile", axis=0, tiled=True),
        lax.all_gather(values, "tile", axis=0, tiled=True),
    )
    group = key_all.shape[0]
    block_count = counts.shape[0]
    block_keys = group // block_count
    slot_index = jnp.arange(group, dtype=jnp.int32) % block_keys
    key_valid = slot_index < jnp.repeat(counts, block_keys)
    tile_count = visible.shape[0]
    tile_rows = row_count // tile_count
    mask_tiles = (jnp.repeat(visible, block_keys, axis=1) == 1) & key_valid[None, :]
    per_step = 2
    step_count = tile_count // per_step
    step_rows = per_step * tile_rows
    query_blocks = queries.reshape(step_count, step_rows, H, head_dim)
    grad_blocks = grad_out.reshape(step_count, step_rows, H, head_dim)
    mask_blocks = mask_tiles.reshape(step_count, per_step, group)
    key_heads = key_all.reshape(group, H, head_dim)
    value_heads = value_all.reshape(group, H, head_dim)

    def scores_of(query_blk, key_mat):
        return (
            jnp.einsum("qhd,khd->hqk", query_blk, key_mat, preferred_element_type=jnp.float32)
            * scale
        )

    def row_mask(mask_blk):
        return jnp.repeat(mask_blk, tile_rows, axis=0)[None, :, :]

    def local_stats(inputs):
        query_blk, mask_blk = inputs
        scores = scores_of(query_blk, key_heads)
        allowed = row_mask(mask_blk)
        top = jnp.max(jnp.where(allowed, scores, -1e30), axis=-1)
        total = jnp.sum(jnp.where(allowed, jnp.exp(scores - top[..., None]), 0.0), axis=-1)
        return (top, total)

    local_top, local_total = lax.map(local_stats, (query_blocks, mask_blocks))
    global_top, global_total = merged((local_top, local_total), "cam", combine_stats)
    lse_all = global_top + jnp.log(global_total)

    def probs_terms(query_blk, grad_blk, mask_blk, lse_blk, key_mat, value_mat):
        scores = scores_of(query_blk, key_mat)
        allowed = row_mask(mask_blk)
        probs = jnp.where(allowed, jnp.exp(scores - lse_blk[..., None]), 0.0)
        dprobs = jnp.einsum("qhd,khd->hqk", grad_blk, value_mat, preferred_element_type=jnp.float32)
        return (probs, dprobs)

    def local_delta(inputs):
        query_blk, grad_blk, mask_blk, lse_blk = inputs
        probs, dprobs = probs_terms(query_blk, grad_blk, mask_blk, lse_blk, key_heads, value_heads)
        return jnp.sum(probs * dprobs, axis=-1)

    delta_part = lax.map(local_delta, (query_blocks, grad_blocks, mask_blocks, lse_all))
    delta_all = lax.psum(delta_part, "cam")

    def rounded_terms(query_blk, grad_blk, mask_blk, lse_blk, delta_blk, key_mat, value_mat):
        probs, dprobs = probs_terms(query_blk, grad_blk, mask_blk, lse_blk, key_mat, value_mat)
        dscores = probs * (dprobs - delta_blk[..., None])
        return (probs.astype(jnp.bfloat16), dscores.astype(jnp.bfloat16))

    def query_grad_of(dscores_b):
        grad_q = (
            jnp.einsum("hqk,khd->qhd", dscores_b, key_heads, preferred_element_type=jnp.float32)
            * scale
        )
        return grad_q.reshape(step_rows, width)

    def grad_step(carry, inputs):
        query_blk, grad_blk, mask_blk, lse_blk, delta_blk = inputs
        probs_b, dscores_b = rounded_terms(
            query_blk, grad_blk, mask_blk, lse_blk, delta_blk, key_heads, value_heads
        )
        grad_k = (
            carry[0]
            + jnp.einsum("hqk,qhd->khd", dscores_b, query_blk, preferred_element_type=jnp.float32)
            * scale
        )
        grad_v = carry[1] + jnp.einsum(
            "hqk,qhd->khd", probs_b, grad_blk, preferred_element_type=jnp.float32
        )
        return ((grad_k, grad_v), query_grad_of(dscores_b))

    zero_kv = jnp.zeros((group, H, head_dim), jnp.float32)
    (grad_k, grad_v), query_parts = lax.scan(
        grad_step, (zero_kv, zero_kv), (query_blocks, grad_blocks, mask_blocks, lse_all, delta_all)
    )
    joined = jnp.concatenate((grad_k.reshape(group, width), grad_v.reshape(group, width)), axis=1)
    owned = lax.psum_scatter(joined, "tile", scatter_dimension=0, tiled=True)
    grad_queries = lax.psum(query_parts.reshape(row_count, width), "cam").astype(jnp.bfloat16)
    grad_keys = owned[:, :width].astype(jnp.bfloat16)
    grad_values = owned[:, width:].astype(jnp.bfloat16)
    return (grad_queries, grad_keys, grad_values)


def solution(mesh):
    in_specs = (
        P("tile", None),
        P(("cam", "tile"), None),
        P(("cam", "tile"), None),
        P("tile", None),
        P("tile", "cam"),
        P("cam"),
    )
    out_specs = (P("tile", None), P(("cam", "tile"), None), P(("cam", "tile"), None))
    return jax.shard_map(shards, mesh=mesh, in_specs=in_specs, out_specs=out_specs, check_vma=False)
```

profile of v0, /device:TPU:0, one launch (start us, length us, event | category | flops | bytes accessed | tf_op | source)
XLA Modules:
  0.0 218.7 jit_solution(8810301855245995741)
XLA Ops:
  7.2 0.0 reduce-scatter.2.cloned.1.call-start
  7.2 0.7 broadcast_in_dim.79
  7.9 0.1 reshape.121
  8.0 0.7 broadcast_compare_fusion
  8.7 0.1 broadcast_in_dim.78
  8.8 0.1 eq.14
  8.9 45.6 %all_gather.18 = bf16[1024,256]{1,0:T(8,128)(2,1)S(1)} all-gather(bf16[64,256]{1,0:T(8,128)(2,1)} %param.7), channel_id=1, replica_groups=mesh['cam'=2,'tile'=16] {'tile'}, dimensions={0}, use_global_device_ids=true | all-gather | bytes 557056 | tf_op jit(solution)/shard_map/all_gather | solution.py:31
  54.4 0.2 copy.19
  54.7 1.0 copy.18
  55.7 0.1 broadcast_in_dim.80
  55.8 0.0 copy-start.3
  55.8 0.0 copy-start.4
  55.8 1.7 select_reduce_fusion.1
  57.5 0.0 copy-start
  57.5 1.8 all-gather
  59.3 1.4 copy-done
  60.7 2.4 %select_reduce_fusion = f32[8,256]{1,0:T(8,128)S(1)} fusion(f32[8,256,1024]{2,1,0:T(8,128)S(1)} %get-tuple-element.69, f32[8,256]{1,0:T(8,128)S(1)} %get-tuple-element.68, pred[256,1024]{1,0:T(8,128)(4,1)S(1)} %bitcast.24), kind=kLoop, calls=%fused_computation.3 | loop fusion | flops 8386560 | bytes 8667136 | tf_op jit(solution)/shard_map/while/body/eval_jaxpr/reduce_sum | solution.py:65
  63.1 1.8 all-gather.1
  64.9 0.0 copy-done.3
  64.9 0.1 copy.20
  65.0 0.0 copy-done.4
  65.1 38.3 %all_gather.23 = bf16[1024,256]{1,0:T(8,128)(2,1)S(1)} all-gather(bf16[64,256]{1,0:T(8,128)(2,1)S(1)} %copy-done.4), channel_id=1, replica_groups=mesh['cam'=2,'tile'=16] {'tile'}, dimensions={0}, use_global_device_ids=true | all-gather | bytes 557056 | tf_op jit(solution)/shard_map/all_gather | solution.py:32
  103.3 0.2 copy.21
  103.5 0.0 copy-start.1
  103.6 5.7 %fusion.1 = f32[8,1024,32]{1,2,0:T(8,128)} fusion(bf16[256,8,32]{0,2,1:T(8,128)(2,1)S(1)} %bitcast.36, f32[8,256,1024]{2,1,0:T(8,128)} %copy-done, f32[8,256]{1,0:T(8,128)S(1)} %fusion.6, pred[256,1024]{1,0:T(8,128)(4,1)S(1)} %bitcast.25), kind=kOutput, calls=%fused_computation.6 | convolution fusion | flops 142606336 | bytes 9838592 | tf_op jit(solution)/shard_map/while/body/eval_jaxpr/hqk,qhd->khd/dot_general | solution.py:109
  109.3 0.3 copy-done.1
  109.6 5.4 %multiply_reduce_fusion = (f32[8,256]{1,0:T(8,128)S(1)}, f32[8,256,1024]{2,1,0:T(8,128)}) fusion(f32[8,256,1024]{2,1,0:T(8,128)S(1)} %copy-done.1, f32[8,256]{1,0:T(8,128)S(1)} %fusion.6, pred[256,1024]{1,0:T(8,128)(4,1)S(1)} %bitcast.26, bf16[256,8,32]{0,2,1:T(8,128)(2,1)S(1)} %bitcast.37, bf16[1024,8,32]{0,2,1:T(8,128)(2,1)S(1)} %bitcast.31), kind=kOutput, calls=%fused_computation.1 | convolution fusion | flops 144701440 | bytes 17711104 | tf_op jit(solution)/shard_map/while/body/eval_jaxpr/qhd,khd->hqk/dot_general | solution.py:76
  114.9 2.5 %psum.14 = f32[8,256]{1,0:T(8,128)S(1)} all-reduce(f32[8,256]{1,0:T(8,128)S(1)} %get-tuple-element.70), channel_id=1, replica_groups=mesh['cam'=2,'tile'=16] {'cam'}, use_global_device_ids=true, to_apply=%region_3.4 | all-reduce | flops 2048 | bytes 16384 | tf_op jit(solution)/shard_map/psum | solution.py:85
  117.4 7.1 %multiply_convert_fusion = bf16[8,256,1024]{2,1,0:T(8,128)(2,1)S(1)} fusion(f32[8,256,1024]{2,1,0:T(8,128)} %get-tuple-element.71, f32[8,256,1024]{2,1,0:T(8,128)} %copy-done, f32[8,256]{1,0:T(8,128)S(1)} %psum.14, f32[8,256]{1,0:T(8,128)S(1)} %fusion.6, pred[256,1024]{1,0:T(8,128)(4,1)S(1)} %bitcast.27), kind=kLoop, calls=%fused_computation | loop fusion | flops 12582912 | bytes 21250048 | tf_op jit(solution)/shard_map/while/body/eval_jaxpr/convert_element_type | solution.py:90
  124.5 0.0 copy-start.2
  124.5 1.9 copy-done.2
  126.4 0.8 convolution_multiply_fusion
  127.2 0.3 copy.23
  127.6 1.6 copy.24
  129.1 1.7 pad_maximum_fusion
  130.8 0.0 reduce-scatter.2.cloned.1.call-update
  130.8 3.5 %convolution_multiply_fusion.1 = f32[8,256,32]{1,2,0:T(8,128)S(1)} fusion(bf16[8,256,1024]{2,1,0:T(8,128)(2,1)} %copy-done.2, bf16[1024,8,32]{0,2,1:T(8,128)(2,1)S(1)} %bitcast.29), kind=kOutput, calls=%fused_computation.10 | convolution fusion | flops 134283264 | bytes 4980736 | tf_op jit(solution)/shard_map/while/body/eval_jaxpr/hqk,khd->qhd/dot_general | solution.py:94
  134.3 0.1 copy.22
  134.5 4.7 %all-reduce.1 = bf16[256,256]{1,0:T(8,128)(2,1)} all-reduce(f32[256,256]{1,0:T(8,128)S(1)} %copy.22), channel_id=1, replica_groups=mesh['cam'=2,'tile'=16] {'cam'}, use_global_device_ids=true, to_apply=%region_4.5 | all-reduce | flops 65536 | bytes 393216 | tf_op jit(solution)/shard_map/psum | solution.py:120
  139.2 71.1 %reduce-scatter.2.cloned.1.call-done = f32[64,512]{1,0:T(8,128)} async-done(((f32[1024,512]{1,0:T(8,128)}), f32[64,512]{1,0:T(8,128)}) %reduce-scatter.2.cloned.1.call-update) | async-done | bytes 131088 | tf_op jit(solution)/shard_map/reduce_scatter | solution.py:119
  210.3 0.9 convert.4
  211.2 0.6 fusion.14
  (3 shorter events, 0.0 us)
Async XLA Ops:
  7.2 203.2 %reduce-scatter.2.cloned.1.call-start = ((), (), s32[]{:S(2)}) async-start(), calls=%async_computation.1 | async-start | bytes 2228224 | tf_op jit(solution)/shard_map/reduce_scatter | solution.py:119
  55.8 9.2 %copy-start.3 = (bf16[256,256]{1,0:T(8,128)(2,1)S(1)}, bf16[256,256]{1,0:T(8,128)(2,1)}, u32[]{:S(2)}) copy-start(bf16[256,256]{1,0:T(8,128)(2,1)} %param.9) | copy-start | bytes 393220
  55.8 9.3 %copy-start.4 = (bf16[64,256]{1,0:T(8,128)(2,1)S(1)}, bf16[64,256]{1,0:T(8,128)(2,1)}, u32[]{:S(2)}) copy-start(bf16[64,256]{1,0:T(8,128)(2,1)} %param.8) | copy-start | bytes 98308
  57.5 3.2 %copy-start = (f32[8,256,1024]{2,1,0:T(8,128)}, f32[8,256,1024]{2,1,0:T(8,128)S(1)}, u32[]{:S(2)}) copy-start(f32[8,256,1024]{2,1,0:T(8,128)S(1)} %get-tuple-element.69) | copy-start | bytes 25165828
  103.5 6.0 %copy-start.1 = (f32[8,256,1024]{2,1,0:T(8,128)S(1)}, f32[8,256,1024]{2,1,0:T(8,128)}, u32[]{:S(2)}) copy-start(f32[8,256,1024]{2,1,0:T(8,128)} %copy-done) | copy-start | bytes 25165828
  124.5 1.9 copy-start.2
Sparse Core Ops, SparseCore 0:
  130.9 79.3 reduce-scatter.1
where the time goes:
time: 219 us
  blocking collectives  94.6 us (43%)
  waiting for transfers between devices  71.2 us (33%)
  matrix products  17.1 us (8%)
  between operations  14.2 us (6%)
  other arithmetic  12.8 us (6%)
  local copies, waits for them, and re-layouts  8.84 us (4%)
    reduce_scatter x1, waiting for transfers between devices, shards(): owned = lax.psum_scatter(joined, 'tile', scatter_dimension=0, tiled=True)  71.1 us
    all_gather x1, blocking collectives, shards(): lax.all_gather(keys, 'tile', axis=0, tiled=True)  45.6 us
    all_gather x1, blocking collectives, shards(): lax.all_gather(values, 'tile', axis=0, tiled=True)  38.3 us
    convert_element_type x1, other arithmetic, rounded_terms(): return (probs.astype(jnp.bfloat16), dscores.astype(jnp.bfloat16))  7.09 us
    dot_general x1, matrix products, grad_step(): jnp.einsum('hqk,qhd->khd', probs_b, grad_blk, preferred_element_type=jnp....  5.71 us
    dot_general x1, matrix products, probs_terms(): jnp.einsum('qhd,khd->hqk', grad_blk, value_mat, preferred_element_type=jn...  5.35 us
    unnamed x12, local copies, waits for them, and re-layouts  4.72 us
    psum x1, blocking collectives, shards(): lax.psum(query_parts.reshape(row_count, width), 'cam').astype(jnp.bfloat16)  4.69 us
  transfers between devices with their start and end apart: 1, of which 1 were waited for; matrix products, arithmetic and copies ran while one was open for 2% of the time, Pallas kernels for 0%

commit v1 on v0

--- a/solution.py
+++ b/solution.py
@@ -5,6 +5,18 @@
 from jax.sharding import PartitionSpec as P
 
 H = 8
+
+
+def doubled_up(value, axis, dim):
+    ways, here = (lax.axis_size(axis), lax.axis_index(axis))
+    grown, reach = (value, 1)
+    while reach < ways:
+        theirs = lax.ppermute(grown, axis, [(d, d ^ reach) for d in range(ways)])
+        mine_first = jnp.concatenate([grown, theirs], axis=dim)
+        theirs_first = jnp.concatenate([theirs, grown], axis=dim)
+        grown = jnp.where(here & reach == 0, mine_first, theirs_first)
+        reach = 2 * reach
+    return grown
 
 
 def merged(array, axis, combine):
@@ -28,7 +40,7 @@
     head_dim = width // H
     scale = 1.0 / math.sqrt(head_dim)
     key_all, value_all = (
-        lax.all_gather(keys, "tile", axis=0, tiled=True),
+        doubled_up(keys, "tile", 0),
         lax.all_gather(values, "tile", axis=0, tiled=True),
     )
     group = key_all.shape[0]

time: 219 us -> 186 us (0.85)
  blocking collectives: 94.6 us -> 54.5 us
  starting transfers between devices: 0.04 us -> 7.04 us
  waiting for transfers between devices: 71.2 us -> 77.3 us
  matrix products: 17.1 us -> 12.5 us
    all_gather x1 -> x0, blocking collectives: 45.6 us -> none  [shards(): lax.all_gather(keys, 'tile', axis=0, tiled=True)]
    ppermute x0 -> x4, waiting for transfers between devices: none -> 7.54 us  [doubled_up(): theirs = lax.ppermute(grown, axis, [(d, d ^ reach) for d in range(ways)])]
    ppermute x0 -> x4, starting transfers between devices: none -> 7.01 us  [doubled_up(): theirs = lax.ppermute(grown, axis, [(d, d ^ reach) for d in range(ways)])]
    all_gather x1, blocking collectives: 38.3 us -> 43.7 us  [shards(): lax.all_gather(values, 'tile', axis=0, tiled=True)]
    dot_general x1, matrix products: 5.71 us -> 1.78 us  [grad_step(): jnp.einsum('hqk,qhd->khd', probs_b, grad_blk, preferred_element_type=jnp....]
    unnamed x12 -> x9, local copies, waits for them, and re-layouts: 4.72 us -> 4.81 us
  transfers between devices with their start and end apart: 1 -> 5, of which waited for: 1 -> 3; matrix products, arithmetic and copies ran while one was open for 2% -> 4% of each run, Pallas kernels for 0% -> 0%
where the time goes in v1:
time: 186 us
  waiting for transfers between devices  77.3 us (42%)
  blocking collectives  54.5 us (29%)
  between operations  14.2 us (8%)
  other arithmetic  12.6 us (7%)
  matrix products  12.5 us (7%)
  local copies, waits for them, and re-layouts  7.93 us (4%)
  starting transfers between devices  7.04 us (4%)
    reduce_scatter x1, waiting for transfers between devices, shards(): owned = lax.psum_scatter(joined, 'tile', scatter_dimension=0, tiled=True)  69.7 us
    all_gather x1, blocking collectives, shards(): lax.all_gather(values, 'tile', axis=0, tiled=True)  43.7 us
    ppermute x4, waiting for transfers between devices, doubled_up(): theirs = lax.ppermute(grown, axis, [(d, d ^ reach) for d in range(ways)])  7.54 us
    convert_element_type x1, other arithmetic, rounded_terms(): return (probs.astype(jnp.bfloat16), dscores.astype(jnp.bfloat16))  7.04 us
    ppermute x4, starting transfers between devices, doubled_up(): theirs = lax.ppermute(grown, axis, [(d, d ^ reach) for d in range(ways)])  7.01 us
    unnamed x9, local copies, waits for them, and re-layouts  4.81 us
    dot_general x1, matrix products, probs_terms(): jnp.einsum('qhd,khd->hqk', grad_blk, value_mat, preferred_element_type=jn...  4.76 us
    psum x1, blocking collectives, shards(): lax.psum(query_parts.reshape(row_count, width), 'cam').astype(jnp.bfloat16)  4.68 us
  transfers between devices with their start and end apart: 5, of which 3 were waited for; matrix products, arithmetic and copies ran while one was open for 4% of the time, Pallas kernels for 0%

profile of v1, /device:TPU:0, one launch (start us, length us, event | category | flops | bytes accessed | tf_op | source)
XLA Modules:
  0.0 186.1 jit_solution(17042301557115963959)
XLA Ops:
  7.2 0.0 reduce-scatter.2.cloned.1.call-start
  7.2 0.9 copy.33
  8.1 3.0 %collective-permute-start = (bf16[64,256]{0,1:T(8,128)(2,1)S(1)}, bf16[64,256]{0,1:T(8,128)(2,1)S(1)}, u32[]{:S(2)}, u32[]{:S(2)}) collective-permute-start(bf16[64,256]{0,1:T(8,128)(2,1)S(1)} %copy.33), channel_id=1, source_target_pairs={{0,1},{1,0},{2,3},{3,2},{4,5},{5,4},{6,7},{7,6},{8,9},{9,8},{10,11... | collective-permute-start | bytes 98312 | tf_op jit(solution)/shard_map/ppermute | solution.py:14
  11.1 0.7 broadcast_in_dim.79
  11.8 0.1 reshape.135
  11.9 0.7 broadcast_compare_fusion
  12.6 0.1 broadcast_in_dim.78
  12.7 0.1 eq.30
  12.8 0.6 collective-permute-done
  13.4 0.1 maximum_select_fusion.8
  13.5 2.1 %collective-permute-start.1 = (bf16[128,256]{0,1:T(8,128)(2,1)S(1)}, bf16[128,256]{0,1:T(8,128)(2,1)S(1)}, u32[]{:S(2)}, u32[]{:S(2)}) collective-permute-start(bf16[128,256]{0,1:T(8,128)(2,1)S(1)} %maximum_select_fusion.8), channel_id=1, source_target_pairs={{0,2},{1,3},{2,0},{3,1},{4,6},{5,7},{6,4},{7,5},{8,10},{9,11},{10,... | collective-permute-start | bytes 196616 | tf_op jit(solution)/shard_map/ppermute | solution.py:14
  15.6 0.1 broadcast_in_dim.80
  15.7 0.4 copy.37
  16.2 1.0 copy.38
  17.2 1.0 copy.39
  18.2 0.0 collective-permute-done.1
  18.2 1.8 collective-permute-start.2
  20.0 43.7 %all_gather.19 = bf16[1024,256]{1,0:T(8,128)(2,1)S(1)} all-gather(bf16[64,256]{1,0:T(8,128)(2,1)} %param.8), channel_id=1, replica_groups=mesh['cam'=2,'tile'=16] {'tile'}, dimensions={0}, use_global_device_ids=true | all-gather | bytes 557056 | tf_op jit(solution)/shard_map/all_gather | solution.py:44
  63.7 0.2 copy.40
  63.9 0.0 collective-permute-done.2
  63.9 0.1 maximum_select_fusion.2
  64.1 0.1 collective-permute-start.3
  64.1 0.1 maximum_select_fusion.7
  64.3 0.1 maximum_select_fusion.1
  64.4 7.0 %collective-permute-done.3 = bf16[512,256]{0,1:T(8,128)(2,1)S(1)} collective-permute-done((bf16[512,256]{0,1:T(8,128)(2,1)S(1)}, bf16[512,256]{0,1:T(8,128)(2,1)S(1)}, u32[]{:S(2)}, u32[]{:S(2)}) %collective-permute-start.3) | collective-permute-done | bytes 262176 | tf_op jit(solution)/shard_map/ppermute | solution.py:14
  71.4 1.6 fusion
  73.0 0.0 copy-start
  73.0 1.8 all-gather
  74.8 1.7 fusion.3
  76.5 1.8 all-gather.1
  78.4 1.8 fusion.7
  80.1 0.0 copy-done
  80.2 4.8 %multiply_reduce_fusion = (f32[8,256]{1,0:T(8,128)S(1)}, f32[8,256,1024]{1,2,0:T(8,128)}) fusion(f32[8,1024,256]{2,1,0:T(8,128)S(1)} %get-tuple-element.69, f32[8,256]{1,0:T(8,128)S(1)} %fusion.13, pred[256,1024]{0,1:T(8,128)(4,1)S(1)} %copy.37, bf16[256,8,32]{0,2,1:T(8,128)(2,1)S(1)} %bitcast.55, bf16[1024,8,32]{0,2,1:T(8,128)(2,1)S(1)} %bitcast.49), kind=kOutput, calls=%fused_computation.10 | convolution fusion | flops 144701440 | bytes 17711104 | tf_op jit(solution)/shard_map/while/body/eval_jaxpr/qhd,khd->hqk/dot_general | solution.py:88
  84.9 2.5 %psum.14 = f32[8,256]{1,0:T(8,128)S(1)} all-reduce(f32[8,256]{1,0:T(8,128)S(1)} %get-tuple-element.70), channel_id=1, replica_groups=mesh['cam'=2,'tile'=16] {'cam'}, use_global_device_ids=true, to_apply=%region_3.4 | all-reduce | flops 2048 | bytes 16384 | tf_op jit(solution)/shard_map/psum | solution.py:97
  87.4 0.0 copy-done.2
  87.4 7.0 %multiply_convert_fusion = bf16[8,256,1024]{1,2,0:T(8,128)(2,1)S(1)} fusion(f32[8,256,1024]{1,2,0:T(8,128)} %get-tuple-element.71, f32[8,1024,256]{2,1,0:T(8,128)} %copy-done, f32[8,256]{1,0:T(8,128)S(1)} %psum.14, f32[8,256]{1,0:T(8,128)S(1)} %fusion.13, pred[256,1024]{0,1:T(8,128)(4,1)S(1)} %copy.37), kind=kLoop, calls=%fused_computation.9 | loop fusion | flops 12582912 | bytes 21250048 | tf_op jit(solution)/shard_map/while/body/eval_jaxpr/convert_element_type | solution.py:102
  94.4 1.9 %copy-done.1 = bf16[8,256,1024]{1,2,0:T(8,128)(2,1)} copy-done((bf16[8,256,1024]{1,2,0:T(8,128)(2,1)}, bf16[8,256,1024]{1,2,0:T(8,128)(2,1)S(1)}, u32[]{:S(2)}) %copy-start.1) | copy-done | bytes 4194328
  96.4 1.3 convolution_multiply_fusion
  97.7 0.3 copy.47
  98.0 0.3 copy.48
  98.4 1.7 pad_maximum_fusion
  100.0 0.0 reduce-scatter.2.cloned.1.call-update
  100.0 3.1 %convolution_multiply_fusion.1 = f32[8,32,256]{2,1,0:T(8,128)S(1)} fusion(bf16[8,256,1024]{1,2,0:T(8,128)(2,1)} %copy-done.1, bf16[512,8,32]{0,2,1:T(8,128)(2,1)} %bitcast.60, bf16[512,8,32]{0,2,1:T(8,128)(2,1)S(1)} %maximum_select_fusion.1, pred[]{:T(512)S(6)} %eq.24), kind=kOutput, calls=%fused_computation.16 | convolution fusion | flops 136642560 | bytes 4980737 | tf_op jit(solution)/shard_map/while/body/eval_jaxpr/hqk,khd->qhd/dot_general | solution.py:106
  103.2 0.1 copy.44
  103.3 4.7 %all-reduce.1 = bf16[256,256]{1,0:T(8,128)(2,1)} all-reduce(f32[256,256]{1,0:T(8,128)S(1)} %copy.44), channel_id=1, replica_groups=mesh['cam'=2,'tile'=16] {'cam'}, use_global_device_ids=true, to_apply=%region_4.5 | all-reduce | flops 65536 | bytes 393216 | tf_op jit(solution)/shard_map/psum | solution.py:132
  108.0 69.7 %reduce-scatter.2.cloned.1.call-done = f32[64,512]{1,0:T(8,128)} async-done(((f32[1024,512]{1,0:T(8,128)}), f32[64,512]{1,0:T(8,128)}) %reduce-scatter.2.cloned.1.call-update) | async-done | bytes 131088 | tf_op jit(solution)/shard_map/reduce_scatter | solution.py:131
  177.7 0.9 convert.4
  178.6 0.6 fusion.23
  (7 shorter events, 0.1 us)
Async XLA Ops:
  7.2 170.5 %reduce-scatter.2.cloned.1.call-start = ((), (), s32[]{:S(2)}) async-start(), calls=%async_computation.1 | async-start | bytes 2228224 | tf_op jit(solution)/shard_map/reduce_scatter | solution.py:131
  8.1 5.3 %collective-permute-start = (bf16[64,256]{0,1:T(8,128)(2,1)S(1)}, bf16[64,256]{0,1:T(8,128)(2,1)S(1)}, u32[]{:S(2)}, u32[]{:S(2)}) collective-permute-start(bf16[64,256]{0,1:T(8,128)(2,1)S(1)} %copy.33), channel_id=1, source_target_pairs={{0,1},{1,0},{2,3},{3,2},{4,5},{5,4},{6,7},{7,6},{8,9},{9,8},{10,11... | collective-permute-start | bytes 98312 | tf_op jit(solution)/shard_map/ppermute | solution.py:14
  13.5 4.7 %collective-permute-start.1 = (bf16[128,256]{0,1:T(8,128)(2,1)S(1)}, bf16[128,256]{0,1:T(8,128)(2,1)S(1)}, u32[]{:S(2)}, u32[]{:S(2)}) collective-permute-start(bf16[128,256]{0,1:T(8,128)(2,1)S(1)} %maximum_select_fusion.8), channel_id=1, source_target_pairs={{0,2},{1,3},{2,0},{3,1},{4,6},{5,7},{6,4},{7,5},{8,10},{9,11},{10,... | collective-permute-start | bytes 196616 | tf_op jit(solution)/shard_map/ppermute | solution.py:14
  18.2 45.7 %collective-permute-start.2 = (bf16[256,256]{0,1:T(8,128)(2,1)S(1)}, bf16[256,256]{0,1:T(8,128)(2,1)S(1)}, u32[]{:S(2)}, u32[]{:S(2)}) collective-permute-start(bf16[256,256]{0,1:T(8,128)(2,1)S(1)} %maximum_select_fusion.4), channel_id=1, source_target_pairs={{0,4},{1,5},{2,6},{3,7},{4,0},{5,1},{6,2},{7,3},{8,12},{9,13},{10,... | collective-permute-start | bytes 393224 | tf_op jit(solution)/shard_map/ppermute | solution.py:14
  64.1 7.3 %collective-permute-start.3 = (bf16[512,256]{0,1:T(8,128)(2,1)S(1)}, bf16[512,256]{0,1:T(8,128)(2,1)S(1)}, u32[]{:S(2)}, u32[]{:S(2)}) collective-permute-start(bf16[512,256]{0,1:T(8,128)(2,1)S(1)} %maximum_select_fusion.2), channel_id=1, source_target_pairs={{0,8},{1,9},{2,10},{3,11},{4,12},{5,13},{6,14},{7,15},{8,0},{9,1},... | collective-permute-start | bytes 786440 | tf_op jit(solution)/shard_map/ppermute | solution.py:14
  71.4 16.0 %copy-start.2 = (bf16[512,256]{0,1:T(8,128)(2,1)}, bf16[512,256]{0,1:T(8,128)(2,1)S(1)}, u32[]{:S(2)}) copy-start(bf16[512,256]{0,1:T(8,128)(2,1)S(1)} %collective-permute-done.3) | copy-start | bytes 786436
  73.0 7.2 %copy-start = (f32[8,1024,256]{2,1,0:T(8,128)}, f32[8,1024,256]{2,1,0:T(8,128)S(1)}, u32[]{:S(2)}) copy-start(f32[8,1024,256]{2,1,0:T(8,128)S(1)} %get-tuple-element.69) | copy-start | bytes 25165828
  94.4 1.9 %copy-start.1 = (bf16[8,256,1024]{1,2,0:T(8,128)(2,1)}, bf16[8,256,1024]{1,2,0:T(8,128)(2,1)S(1)}, u32[]{:S(2)}) copy-start(bf16[8,256,1024]{1,2,0:T(8,128)(2,1)S(1)} %multiply_convert_fusion) | copy-start | bytes 12582916
Sparse Core Ops, SparseCore 0:
  100.2 77.4 reduce-scatter.1
